TPU v7x, 32 devices: a whole 2x2x4 slice. The times are simulated.
32 devices in a mesh: dp: 8 (over z, y), tensor: 4 (over x, core).
Axes of the slice: x: 2, y: 2, z: 4, core: 2. Of those that a mesh axis runs over, the one named last changes fastest.
Arguments:
- tokens: bfloat16 [16384, 512], P(('dp', 'tensor')), may hold values from -6 to 6
- encoder_states: bfloat16 [16384, 512], P(('dp', 'tensor')), may hold values from -6 to 6
- output_grad: bfloat16 [16384, 512], P(('dp', 'tensor')), may hold values from -6 to 6
- valid_mask: int32 [16384], P(('dp', 'tensor')), may hold values 0 or 1
- segment_ids: int32 [16, 1024], P('dp'), may hold values from 0 to 15, never falling along the last dimension, each value on 1 to 512 neighbouring positions
- context_ranks: int32 [16, 8], P('dp'), may hold values from 0 to 7, each once within a row
- self_query: bfloat16 [512, 512], P('dp', 'tensor'), may hold values from -0.25 to 0.25
- self_key: bfloat16 [512, 512], P('dp', 'tensor'), may hold values from -0.25 to 0.25
- self_value: bfloat16 [512, 512], P('dp', 'tensor'), may hold values from -0.25 to 0.25
- self_output: bfloat16 [512, 512], P('tensor', 'dp'), may hold values from -1.5 to 1.5
- cross_query: bfloat16 [512, 512], P('dp', 'tensor'), may hold values from -0.25 to 0.25
- cross_key: bfloat16 [512, 512], P('dp', 'tensor'), may hold values from -0.25 to 0.25
- cross_value: bfloat16 [512, 512], P('dp', 'tensor'), may hold values from -0.25 to 0.25
- cross_output: bfloat16 [512, 512], P('tensor', 'dp'), may hold values from -4 to 4
- hidden_up: bfloat16 [512, 2048], P('dp', 'tensor'), may hold values from -0.25 to 0.25
- hidden_down: bfloat16 [2048, 512], P('tensor', 'dp'), may hold values from -0.1875 to 0.1875
- norm1_gain: float32 [512], replicated, may hold values from 0.5 to 1.5
- norm1_bias: float32 [512], replicated, may hold values from -1.2 to 1.2
- norm2_gain: float32 [512], replicated, may hold values from 0.5 to 1.5
- norm2_bias: float32 [512], replicated, may hold values from -1.2 to 1.2
- norm3_gain: float32 [512], replicated, may hold values from 0.5 to 1.5
- norm3_bias: float32 [512], replicated, may hold values from -1.2 to 1.2
Outputs:
- layer_output: float32 [16384, 512], P(('dp', 'tensor'))
- tokens_grad: float32 [16384, 512], P(('dp', 'tensor'))
- encoder_grad: float32 [16384, 512], P(('dp', 'tensor'))
- grad_self_query: float32 [512, 512], P('dp', 'tensor')
- grad_self_key: float32 [512, 512], P('dp', 'tensor')
- grad_self_value: float32 [512, 512], P('dp', 'tensor')
- grad_self_output: float32 [512, 512], P('tensor', 'dp')
- grad_cross_query: float32 [512, 512], P('dp', 'tensor')
- grad_cross_key: float32 [512, 512], P('dp', 'tensor')
- grad_cross_value: float32 [512, 512], P('dp', 'tensor')
- grad_cross_output: float32 [512, 512], P('tensor', 'dp')
- grad_hidden_up: float32 [512, 2048], P('dp', 'tensor')
- grad_hidden_down: float32 [2048, 512], P('tensor', 'dp')
- norm_grads: float32 [6, 512], replicated
- valid_scales: float32 [2, 512], replicated
Inputs may be any that keep to these rules, and one draw needn't show every extreme that they name: `segment_ids`: within a sequence the ids never fall; each document has 1 to 512 tokens and one has exactly 512. `context_ranks`: each sequence's row holds every block rank once.
All inputs are finite; a program needn't handle non-finite values. No bound on the sum of `valid_mask` on one device may be relied on, other than what follows from the above.
Results may differ from a plain program's by a relative error of at most 0.024.
The roundings to bfloat16 on the way count: a program that leaves them out, or rounds other values in their place, can miss the bound.
Values may be sent and summed in bfloat16 or wider, within the bound.
A program may use at most 128 MiB of HBM per device.

v0:
```python
import jax
import jax.numpy as jnp
from jax import lax
from jax.sharding import PartitionSpec as P

HEAD = 64
LEN = 1024
BLK = 128
norm_eps = 1e-05
mask_fill = -1000000000.0


def gelu_exact(value):
    return jax.nn.gelu(value, approximate=False)


def gelu_back(preact, upstream):
    return jax.vjp(gelu_exact, preact)[1](upstream)[0]


def layer_norm(value, gain, bias):
    mean = jnp.mean(value, axis=-1, keepdims=True)
    centred = value - mean
    scale = lax.rsqrt(jnp.mean(centred * centred, axis=-1, keepdims=True) + norm_eps)
    normal = centred * scale
    return (normal * gain + bias, normal, scale)


def norm_back(upstream, normal, scale, gain):
    scaled = upstream * gain
    mean_grad = jnp.mean(scaled, axis=-1, keepdims=True)
    mean_cross = jnp.mean(scaled * normal, axis=-1, keepdims=True)
    inward = scale * (scaled - mean_grad - normal * mean_cross)
    return (inward, jnp.sum(upstream * normal, axis=0), jnp.sum(upstream, axis=0))


def context_allowed(segments, ranks, first, count):
    length = segments.shape[0]
    key_block = jnp.arange(length, dtype=jnp.int32) // BLK
    key_rank = jnp.broadcast_to(ranks[:, None], (ranks.shape[0], BLK)).reshape(length)
    query_segment = lax.dynamic_slice_in_dim(segments, first, count)
    query_rank = lax.dynamic_slice_in_dim(key_rank, first, count)
    query_block = (first + jnp.arange(count, dtype=jnp.int32)) // BLK
    same_doc = query_segment[:, None] == segments[None, :]
    earlier = key_rank[None, :] < query_rank[:, None]
    same_block = query_block[:, None] == key_block[None, :]
    return same_doc & (earlier | same_block)


def full_rows(value):
    return lax.all_gather(value, "tensor", axis=0, tiled=True)


def grad_rows(value):
    return lax.all_gather(value, "tensor", axis=0, tiled=True)


def branch_sum(mixed, weight):
    return lax.psum_scatter(
        jnp.dot(mixed, weight, preferred_element_type=jnp.float32),
        "tensor",
        scatter_dimension=0,
        tiled=True,
    )


def back_product(left, weight):
    return lax.dot_general(
        left, weight, (((1,), (1,)), ((), ())), preferred_element_type=jnp.float32
    )


def row_product(left, right):
    return lax.dot_general(
        left, right, (((0,), (0,)), ((), ())), preferred_element_type=jnp.float32
    )


def input_sum(pairs):
    total = None
    for left, weight in pairs:
        portion = back_product(left, weight)
        total = portion if total is None else total + portion
    return lax.psum_scatter(total, "tensor", scatter_dimension=0, tiled=True)


def split_heads(value, count):
    return value.reshape(count, LEN, value.shape[1] // HEAD, HEAD)


def attend_sequence(query, keys, values, segments, ranks, masked):
    length = query.shape[0]
    width = min(length, 512)

    def one_block(index):
        first = index * width
        piece = lax.dynamic_slice_in_dim(query, first, width, 0)
        scores = jnp.einsum("qhd,khd->hqk", piece, keys, preferred_element_type=jnp.float32) * 0.125
        if masked:
            scores = jnp.where(
                context_allowed(segments, ranks, first, width)[None], scores, mask_fill
            )
        top = jnp.max(scores, axis=-1, keepdims=True)
        raised = jnp.exp(scores - top)
        total = jnp.sum(raised, axis=-1, keepdims=True)
        shares = (raised / total).astype(jnp.bfloat16)
        mixed = jnp.einsum("hqk,khd->qhd", shares, values, preferred_element_type=jnp.float32)
        return (mixed.astype(jnp.bfloat16), (top + jnp.log(total))[..., 0])

    mixed, log_total = lax.map(one_block, jnp.arange(length // width, dtype=jnp.int32))
    return (mixed.reshape(query.shape), log_total)


def attend_sequence_back(query, keys, values, segments, ranks, masked, log_total, grad_mixed):
    length = query.shape[0]
    width = min(length, 512)

    def one_block(carry, index):
        key_sum, value_sum = carry
        first = index * width
        piece = lax.dynamic_slice_in_dim(query, first, width, 0)
        grad_piece = lax.dynamic_slice_in_dim(grad_mixed, first, width, 0)
        scores = jnp.einsum("qhd,khd->hqk", piece, keys, preferred_element_type=jnp.float32) * 0.125
        if masked:
            scores = jnp.where(
                context_allowed(segments, ranks, first, width)[None], scores, mask_fill
            )
        shares = jnp.exp(scores - log_total[index][..., None])
        grad_shares = jnp.einsum(
            "qhd,khd->hqk", grad_piece, values, preferred_element_type=jnp.float32
        )
        inner = jnp.sum(shares * grad_shares, axis=-1, keepdims=True)
        grad_scores = (shares * (grad_shares - inner)).astype(jnp.bfloat16)
        grad_query = (
            jnp.einsum("hqk,khd->qhd", grad_scores, keys, preferred_element_type=jnp.float32)
            * 0.125
        )
        key_sum = (
            key_sum
            + jnp.einsum("hqk,qhd->khd", grad_scores, piece, preferred_element_type=jnp.float32)
            * 0.125
        )
        value_sum = value_sum + jnp.einsum(
            "hqk,qhd->khd",
            shares.astype(jnp.bfloat16),
            grad_piece,
            preferred_element_type=jnp.float32,
        )
        return ((key_sum, value_sum), grad_query.astype(jnp.bfloat16))

    zeros = jnp.zeros(keys.shape, jnp.float32)
    (key_sum, value_sum), grad_query = lax.scan(
        one_block, (zeros, zeros), jnp.arange(length // width, dtype=jnp.int32)
    )
    return (
        grad_query.reshape(query.shape),
        key_sum.astype(jnp.bfloat16),
        value_sum.astype(jnp.bfloat16),
    )


def attend_all(query, keys, values, segments, ranks, masked):
    count = query.shape[0] // LEN

    def one_sequence(items):
        return attend_sequence(items[0], items[1], items[2], items[3], items[4], masked)

    mixed, log_total = lax.map(
        one_sequence,
        (
            split_heads(query, count),
            split_heads(keys, count),
            split_heads(values, count),
            segments,
            ranks,
        ),
    )
    return (mixed.reshape(query.shape), log_total)


def attend_back_all(query, keys, values, segments, ranks, masked, log_total, grad_mixed):
    count = query.shape[0] // LEN

    def one_sequence(items):
        return attend_sequence_back(
            items[0], items[1], items[2], items[3], items[4], masked, items[5], items[6]
        )

    grad_query, grad_keys, grad_values = lax.map(
        one_sequence,
        (
            split_heads(query, count),
            split_heads(keys, count),
            split_heads(values, count),
            segments,
            ranks,
            log_total,
            split_heads(grad_mixed, count),
        ),
    )
    return (
        grad_query.reshape(query.shape),
        grad_keys.reshape(keys.shape),
        grad_values.reshape(values.shape),
    )


def shards(
    tokens,
    encoder_states,
    output_grad,
    valid_mask,
    segment_ids,
    context_ranks,
    self_query,
    self_key,
    self_value,
    self_output,
    cross_query,
    cross_key,
    cross_value,
    cross_output,
    hidden_up,
    hidden_down,
    norm1_gain,
    norm1_bias,
    norm2_gain,
    norm2_bias,
    norm3_gain,
    norm3_bias,
):
    (
        self_query,
        self_key,
        self_value,
        self_output,
        cross_query,
        cross_key,
        cross_value,
        cross_output,
        hidden_up,
        hidden_down,
    ) = (
        lax.all_gather(self_query, "dp", axis=0, tiled=True),
        lax.all_gather(self_key, "dp", axis=0, tiled=True),
        lax.all_gather(self_value, "dp", axis=0, tiled=True),
        lax.all_gather(self_output, "dp", axis=1, tiled=True),
        lax.all_gather(cross_query, "dp", axis=0, tiled=True),
        lax.all_gather(cross_key, "dp", axis=0, tiled=True),
        lax.all_gather(cross_value, "dp", axis=0, tiled=True),
        lax.all_gather(cross_output, "dp", axis=1, tiled=True),
        lax.all_gather(hidden_up, "dp", axis=0, tiled=True),
        lax.all_gather(hidden_down, "dp", axis=1, tiled=True),
    )
    tokens_full = full_rows(tokens)
    query = jnp.dot(tokens_full, self_query, preferred_element_type=jnp.float32).astype(
        jnp.bfloat16
    )
    keys = jnp.dot(tokens_full, self_key, preferred_element_type=jnp.float32).astype(jnp.bfloat16)
    values = jnp.dot(tokens_full, self_value, preferred_element_type=jnp.float32).astype(
        jnp.bfloat16
    )
    self_mixed, self_log = attend_all(query, keys, values, segment_ids, context_ranks, True)
    attended = branch_sum(self_mixed, self_output)
    first_out, first_normal, first_scale = layer_norm(
        tokens.astype(jnp.float32) + attended, norm1_gain, norm1_bias
    )
    first_full = full_rows(first_out.astype(jnp.bfloat16))
    encoder_full = full_rows(encoder_states)
    second_query = jnp.dot(first_full, cross_query, preferred_element_type=jnp.float32).astype(
        jnp.bfloat16
    )
    encoder_keys = jnp.dot(encoder_full, cross_key, preferred_element_type=jnp.float32).astype(
        jnp.bfloat16
    )
    encoder_values = jnp.dot(encoder_full, cross_value, preferred_element_type=jnp.float32).astype(
        jnp.bfloat16
    )
    cross_mixed, cross_log = attend_all(
        second_query, encoder_keys, encoder_values, segment_ids, context_ranks, False
    )
    crossed = branch_sum(cross_mixed, cross_output)
    second_out, second_normal, second_scale = layer_norm(
        first_out + crossed, norm2_gain, norm2_bias
    )
    second_low = second_out.astype(jnp.bfloat16)
    feed_input = full_rows(second_low)
    preact = jnp.dot(feed_input, hidden_up, preferred_element_type=jnp.float32)
    activated = gelu_exact(preact).astype(jnp.bfloat16)
    feed_out = branch_sum(activated, hidden_down)
    third_out, third_normal, third_scale = layer_norm(second_out + feed_out, norm3_gain, norm3_bias)
    valid_rows = valid_mask.astype(jnp.float32)[:, None]
    grad_layer = output_grad.astype(jnp.float32) * valid_rows
    grad_third, gain3_grad, bias3_grad = norm_back(
        grad_layer, third_normal, third_scale, norm3_gain
    )
    grad_third_low = grad_third.astype(jnp.bfloat16)
    grad_feed = grad_rows(grad_third_low)
    grad_active = back_product(grad_feed, hidden_down)
    grad_preact = gelu_back(preact, grad_active).astype(jnp.bfloat16)
    up_grad = row_product(feed_input, grad_preact)
    down_grad = row_product(activated, grad_feed)
    grad_second = grad_third + input_sum([(grad_preact, hidden_up)])
    grad_second_in, gain2_grad, bias2_grad = norm_back(
        grad_second, second_normal, second_scale, norm2_gain
    )
    grad_crossed = grad_rows(grad_second_in.astype(jnp.bfloat16))
    cross_output_grad = row_product(cross_mixed, grad_crossed)
    grad_cross_mixed = back_product(grad_crossed, cross_output).astype(jnp.bfloat16)
    grad_second_query, grad_encoder_keys, grad_encoder_values = attend_back_all(
        second_query,
        encoder_keys,
        encoder_values,
        segment_ids,
        context_ranks,
        False,
        cross_log,
        grad_cross_mixed,
    )
    cross_query_grad = row_product(first_full, grad_second_query)
    cross_key_grad = row_product(encoder_full, grad_encoder_keys)
    cross_value_grad = row_product(encoder_full, grad_encoder_values)
    grad_first = grad_second_in + input_sum([(grad_second_query, cross_query)])
    encoder_grad = input_sum([(grad_encoder_keys, cross_key), (grad_encoder_values, cross_value)])
    grad_first_in, gain1_grad, bias1_grad = norm_back(
        grad_first, first_normal, first_scale, norm1_gain
    )
    grad_attended = grad_rows(grad_first_in.astype(jnp.bfloat16))
    self_output_grad = row_product(self_mixed, grad_attended)
    grad_self_mixed = back_product(grad_attended, self_output).astype(jnp.bfloat16)
    grad_query, grad_keys, grad_values = attend_back_all(
        query, keys, values, segment_ids, context_ranks, True, self_log, grad_self_mixed
    )
    self_query_grad = row_product(tokens_full, grad_query)
    self_key_grad = row_product(tokens_full, grad_keys)
    self_value_grad = row_product(tokens_full, grad_values)
    tokens_grad = grad_first_in + input_sum(
        [(grad_query, self_query), (grad_keys, self_key), (grad_values, self_value)]
    )
    (
        self_query_grad,
        self_key_grad,
        self_value_grad,
        self_output_grad,
        cross_query_grad,
        cross_key_grad,
        cross_value_grad,
        cross_output_grad,
        up_grad,
        down_grad,
    ) = (
        lax.psum_scatter(self_query_grad, "dp", scatter_dimension=0, tiled=True),
        lax.psum_scatter(self_key_grad, "dp", scatter_dimension=0, tiled=True),
        lax.psum_scatter(self_value_grad, "dp", scatter_dimension=0, tiled=True),
        lax.psum_scatter(self_output_grad, "dp", scatter_dimension=1, tiled=True),
        lax.psum_scatter(cross_query_grad, "dp", scatter_dimension=0, tiled=True),
        lax.psum_scatter(cross_key_grad, "dp", scatter_dimension=0, tiled=True),
        lax.psum_scatter(cross_value_grad, "dp", scatter_dimension=0, tiled=True),
        lax.psum_scatter(cross_output_grad, "dp", scatter_dimension=1, tiled=True),
        lax.psum_scatter(up_grad, "dp", scatter_dimension=0, tiled=True),
        lax.psum_scatter(down_grad, "dp", scatter_dimension=1, tiled=True),
    )
    norm_sums, square_sums = lax.psum(
        (
            jnp.stack([gain1_grad, bias1_grad, gain2_grad, bias2_grad, gain3_grad, bias3_grad]),
            jnp.stack(
                [
                    jnp.sum(valid_rows * third_out * third_out, axis=0),
                    jnp.sum(valid_rows * tokens_grad * tokens_grad, axis=0),
                ]
            ),
        ),
        ("dp", "tensor"),
    )
    total_tokens = tokens.shape[0] * lax.axis_size("dp") * lax.axis_size("tensor")
    valid_scales = jnp.sqrt(square_sums / total_tokens)
    return (
        third_out,
        tokens_grad,
        encoder_grad,
        self_query_grad,
        self_key_grad,
        self_value_grad,
        self_output_grad,
        cross_query_grad,
        cross_key_grad,
        cross_value_grad,
        cross_output_grad,
        up_grad,
        down_grad,
        norm_sums,
        valid_scales,
    )


def solution(mesh):
    in_specs = (
        P(("dp", "tensor"), None),
        P(("dp", "tensor"), None),
        P(("dp", "tensor"), None),
        P(("dp", "tensor")),
        P("dp", None),
        P("dp", None),
        P("dp", "tensor"),
        P("dp", "tensor"),
        P("dp", "tensor"),
        P("tensor", "dp"),
        P("dp", "tensor"),
        P("dp", "tensor"),
        P("dp", "tensor"),
        P("tensor", "dp"),
        P("dp", "tensor"),
        P("tensor", "dp"),
        P(),
        P(),
        P(),
        P(),
        P(),
        P(),
    )
    out_specs = (
        P(("dp", "tensor"), None),
        P(("dp", "tensor"), None),
        P(("dp", "tensor"), None),
        P("dp", "tensor"),
        P("dp", "tensor"),
        P("dp", "tensor"),
        P("tensor", "dp"),
        P("dp", "tensor"),
        P("dp", "tensor"),
        P("dp", "tensor"),
        P("tensor", "dp"),
        P("dp", "tensor"),
        P("tensor", "dp"),
        P(),
        P(),
    )
    return jax.shard_map(shards, mesh=mesh, in_specs=in_specs, out_specs=out_specs, check_vma=False)
```

profile of v0, /device:TPU:0, one launch (start us, length us, event | category | flops | bytes accessed | tf_op | source)
XLA Modules:
  0.0 1633.0 jit_solution(10567116157558251906)
XLA Ops:
  8.0 32.6 %all_gather.52 = bf16[512,128]{1,0:T(8,128)(2,1)S(1)} all-gather(bf16[64,128]{1,0:T(8,128)(2,1)} %param.44), channel_id=1, replica_groups=mesh['dp'=8,'tensor'=4] {'dp'}, dimensions={0}, use_global_device_ids=true | all-gather | bytes 147456 | tf_op jit(solution)/shard_map/all_gather | solution.py:244
  40.6 30.8 %all_gather.53 = bf16[512,128]{1,0:T(8,128)(2,1)S(1)} all-gather(bf16[64,128]{1,0:T(8,128)(2,1)} %param.45), channel_id=1, replica_groups=mesh['dp'=8,'tensor'=4] {'dp'}, dimensions={0}, use_global_device_ids=true | all-gather | bytes 147456 | tf_op jit(solution)/shard_map/all_gather | solution.py:245
  102.1 32.7 %all_gather.55 = bf16[128,512]{0,1:T(8,128)(2,1)} all-gather(bf16[128,64]{0,1:T(8,128)(2,1)} %param.47), channel_id=1, replica_groups=mesh['dp'=8,'tensor'=4] {'dp'}, dimensions={1}, use_global_device_ids=true | all-gather | bytes 147456 | tf_op jit(solution)/shard_map/all_gather | solution.py:247
  186.1 44.5 %reduce-scatter.28.cloned.1.call-done = f32[512,512]{1,0:T(8,128)} async-done(((f32[2048,512]{1,0:T(8,128)}), f32[512,512]{1,0:T(8,128)}) %reduce-scatter.28.cloned.1.call-update) | async-done | bytes 1048592 | tf_op jit(solution)/shard_map/reduce_scatter | solution.py:59
  326.3 32.5 %all_gather.61 = bf16[128,512]{0,1:T(8,128)(2,1)} all-gather(bf16[128,64]{0,1:T(8,128)(2,1)S(1)} %copy-done.77), channel_id=1, replica_groups=mesh['dp'=8,'tensor'=4] {'dp'}, dimensions={1}, use_global_device_ids=true | all-gather | bytes 147456 | tf_op jit(solution)/shard_map/all_gather | solution.py:251
  397.9 44.6 %reduce-scatter.30.cloned.1.call-done = f32[512,512]{1,0:T(8,128)} async-done(((f32[2048,512]{1,0:T(8,128)}), f32[512,512]{1,0:T(8,128)}) %reduce-scatter.30.cloned.1.call-update) | async-done | bytes 1048592 | tf_op jit(solution)/shard_map/reduce_scatter | solution.py:59
  445.6 31.4 %all_gather.63 = bf16[512,512]{1,0:T(8,128)(2,1)S(1)} all-gather(bf16[64,512]{1,0:T(8,128)(2,1)S(1)} %copy-done.59), channel_id=1, replica_groups=mesh['dp'=8,'tensor'=4] {'dp'}, dimensions={0}, use_global_device_ids=true | all-gather | bytes 589824 | tf_op jit(solution)/shard_map/all_gather | solution.py:252
  477.0 31.7 %all_gather.64 = bf16[512,512]{0,1:T(8,128)(2,1)S(1)} all-gather(bf16[512,64]{0,1:T(8,128)(2,1)S(1)} %copy-done.60), channel_id=1, replica_groups=mesh['dp'=8,'tensor'=4] {'dp'}, dimensions={1}, use_global_device_ids=true | all-gather | bytes 589824 | tf_op jit(solution)/shard_map/all_gather | solution.py:253
  527.0 44.2 %reduce-scatter.32.cloned.1.call-done = f32[512,512]{1,0:T(8,128)} async-done(((f32[2048,512]{1,0:T(8,128)}), f32[512,512]{1,0:T(8,128)}) %reduce-scatter.32.cloned.1.call-update) | async-done | bytes 1048592 | tf_op jit(solution)/shard_map/reduce_scatter | solution.py:59
  611.9 44.6 %reduce-scatter.34.cloned.1.call-done = f32[512,512]{1,0:T(8,128)} async-done(((f32[2048,512]{1,0:T(8,128)}), f32[512,512]{1,0:T(8,128)}) %reduce-scatter.34.cloned.1.call-update) | async-done | bytes 1048592 | tf_op jit(solution)/shard_map/reduce_scatter | solution.py:84
  691.4 45.9 %while.151 = (s32[]{:T(128)}, bf16[2,1024,2,64]{3,2,1,0:T(2,128)(2,1)}, bf16[2,1024,2,64]{1,3,2,0:T(8,128)(2,1)}, bf16[2,1024,2,64]{1,3,2,0:T(8,128)(2,1)}, bf16...) while((s32[]{:T(128)}, ...), condition=%wide.region_30.31_spmd, body=%wide.region_26.30_spmd.sunk | while | flops 684719104 | bytes 40022608 | solution.py:189
  742.6 44.6 %reduce-scatter.36.cloned.1.call-done = f32[512,512]{1,0:T(8,128)} async-done(((f32[2048,512]{1,0:T(8,128)}), f32[512,512]{1,0:T(8,128)}) %reduce-scatter.36.cloned.1.call-update) | async-done | bytes 1048592 | tf_op jit(solution)/shard_map/reduce_scatter | solution.py:84
  822.1 51.9 %while.153 = (s32[]{:T(128)}, bf16[2,1024,2,64]{3,2,1,0:T(2,128)(2,1)}, bf16[2,1024,2,64]{1,3,2,0:T(8,128)(2,1)}, bf16[2,1024,2,64]{1,3,2,0:T(8,128)(2,1)}, bf16...) while((s32[]{:T(128)}, ...), condition=%wide.region_38.39_spmd, body=%wide.region_34.38_spmd.sunk | while | flops 690502656 | bytes 46359340 | solution.py:189
  932.8 39.9 %all-reduce = (f32[6,512]{1,0:T(8,128)}, f32[2,512]{1,0:T(2,128)S(1)}) all-reduce(f32[6,512]{1,0:T(8,128)S(1)} %stack.36, f32[2,512]{1,0:T(2,128)S(1)} %pad_maximum_fusion), channel_id=1, replica_groups=mesh['dp'=8,'tensor'=4] {'dp','tensor'}, use_global_device_ids=true, to_apply=%region_57.58 | all-reduce | flops 4096 | bytes 32768 | tf_op jit(solution)/shard_map/psum | solution.py:363
  996.8 66.7 %reduce-scatter.50.cloned.1.call-done = f32[512,64]{0,1:T(8,128)} async-done(((f32[512,512]{0,1:T(8,128)}), f32[512,64]{0,1:T(8,128)}) %reduce-scatter.50.cloned.1.call-update) | async-done | bytes 131088 | tf_op jit(solution)/shard_map/reduce_scatter | solution.py:361
  1063.6 64.1 %reduce-scatter.46.cloned.1.call-done = f32[128,64]{0,1:T(8,128)} async-done(((f32[128,512]{0,1:T(8,128)}), f32[128,64]{0,1:T(8,128)}) %reduce-scatter.46.cloned.1.call-update) | async-done | bytes 32784 | tf_op jit(solution)/shard_map/reduce_scatter | solution.py:359
  1127.6 64.1 %reduce-scatter.60.cloned.1.call-done = f32[64,128]{1,0:T(8,128)} async-done(((f32[512,128]{1,0:T(8,128)}), f32[64,128]{1,0:T(8,128)}) %reduce-scatter.60.cloned.1.call-update) | async-done | bytes 32784
  1191.7 64.1 %reduce-scatter.44.cloned.1.call-done = f32[64,128]{1,0:T(8,128)} async-done(((f32[512,128]{1,0:T(8,128)}), f32[64,128]{1,0:T(8,128)}) %reduce-scatter.44.cloned.1.call-update) | async-done | bytes 32784 | tf_op jit(solution)/shard_map/reduce_scatter | solution.py:356
  1255.8 64.2 %reduce-scatter.58.cloned.1.call-done = f32[64,128]{1,0:T(8,128)} async-done(((f32[512,128]{1,0:T(8,128)}), f32[64,128]{1,0:T(8,128)}) %reduce-scatter.58.cloned.1.call-update) | async-done | bytes 32784
  1320.0 46.5 %reduce-scatter.40.cloned.1.call-done = f32[512,512]{1,0:T(8,128)} async-done(((f32[2048,512]{1,0:T(8,128)}), f32[512,512]{1,0:T(8,128)}) %reduce-scatter.40.cloned.1.call-update) | async-done | bytes 1048592 | tf_op jit(solution)/shard_map/reduce_scatter | solution.py:84
  1366.5 65.6 %reduce-scatter.42.cloned.1.call-done = f32[128,64]{0,1:T(8,128)} async-done(((f32[128,512]{0,1:T(8,128)}), f32[128,64]{0,1:T(8,128)}) %reduce-scatter.42.cloned.1.call-update) | async-done | bytes 32784 | tf_op jit(solution)/shard_map/reduce_scatter | solution.py:355
  1432.1 64.6 %reduce-scatter.56.cloned.1.call-done = f32[64,128]{1,0:T(8,128)} async-done(((f32[512,128]{1,0:T(8,128)}), f32[64,128]{1,0:T(8,128)}) %reduce-scatter.56.cloned.1.call-update) | async-done | bytes 32784
  1496.7 64.6 %reduce-scatter.52.cloned.1.call-done = f32[64,128]{1,0:T(8,128)} async-done(((f32[512,128]{1,0:T(8,128)}), f32[64,128]{1,0:T(8,128)}) %reduce-scatter.52.cloned.1.call-update) | async-done | bytes 32784
  1561.3 64.4 %reduce-scatter.54.cloned.1.call-done = f32[64,128]{1,0:T(8,128)} async-done(((f32[512,128]{1,0:T(8,128)}), f32[64,128]{1,0:T(8,128)}) %reduce-scatter.54.cloned.1.call-update) | async-done | bytes 32784
  (608 shorter events, 674.7 us)
Async XLA Ops:
  7.2 127.6 %all-gather.8.cloned.1.call-start = ((), (), s32[]{:S(2)}) async-start(), calls=%async_computation.17 | async-start | bytes 2621440 | tf_op jit(solution)/shard_map/all_gather | solution.py:51
  7.9 222.7 %reduce-scatter.28.cloned.1.call-start = ((), (), s32[]{:S(2)}) async-start(), calls=%async_computation.18 | async-start | bytes 5242880 | tf_op jit(solution)/shard_map/reduce_scatter | solution.py:59
  185.1 173.7 %all-gather.12.cloned.1.call-start = ((), (), s32[]{:S(2)}) async-start(), calls=%async_computation.20 | async-start | bytes 2621440 | tf_op jit(solution)/shard_map/all_gather | solution.py:51
  185.8 182.2 %all-gather.10.cloned.1.call-start = ((), (), s32[]{:S(2)}) async-start(), calls=%async_computation.19 | async-start | bytes 2621440 | tf_op jit(solution)/shard_map/all_gather | solution.py:51
  234.6 208.0 %reduce-scatter.30.cloned.1.call-start = ((), (), s32[]{:S(2)}) async-start(), calls=%async_computation.21 | async-start | bytes 5242880 | tf_op jit(solution)/shard_map/reduce_scatter | solution.py:59
  397.9 110.8 %all-gather.14.cloned.1.call-start = ((), (), s32[]{:S(2)}) async-start(), calls=%async_computation.22 | async-start | bytes 2621440 | tf_op jit(solution)/shard_map/all_gather | solution.py:51
  445.5 125.7 %reduce-scatter.32.cloned.1.call-start = ((), (), s32[]{:S(2)}) async-start(), calls=%async_computation.23 | async-start | bytes 5242880 | tf_op jit(solution)/shard_map/reduce_scatter | solution.py:59
  526.4 74.1 %all-gather.16.cloned.1.call-start = ((), (), s32[]{:S(2)}) async-start(), calls=%async_computation.24 | async-start | bytes 2621440 | tf_op jit(solution)/shard_map/all_gather | solution.py:55
  577.7 78.8 %reduce-scatter.34.cloned.1.call-start = ((), (), s32[]{:S(2)}) async-start(), calls=%async_computation.25 | async-start | bytes 5242880 | tf_op jit(solution)/shard_map/reduce_scatter | solution.py:84
  611.8 71.8 %all-gather.18.cloned.1.call-start = ((), (), s32[]{:S(2)}) async-start(), calls=%async_computation.26 | async-start | bytes 2621440 | tf_op jit(solution)/shard_map/all_gather | solution.py:55
  660.9 126.4 %reduce-scatter.36.cloned.1.call-start = ((), (), s32[]{:S(2)}) async-start(), calls=%async_computation.27 | async-start | bytes 5242880 | tf_op jit(solution)/shard_map/reduce_scatter | solution.py:84
  742.6 71.4 %all-gather.20.cloned.1.call-start = ((), (), s32[]{:S(2)}) async-start(), calls=%async_computation.28 | async-start | bytes 2621440 | tf_op jit(solution)/shard_map/all_gather | solution.py:55
  791.3 138.1 %reduce-scatter.38.cloned.1.call-start = ((), (), s32[]{:S(2)}) async-start(), calls=%async_computation.29 | async-start | bytes 5242880 | tf_op jit(solution)/shard_map/reduce_scatter | solution.py:84
  884.8 112.1 %reduce-scatter.48.cloned.1.call-start = ((), (), s32[]{:S(2)}) async-start(), calls=%async_computation.34 | async-start | bytes 1179648 | tf_op jit(solution)/shard_map/reduce_scatter | solution.py:360
  889.7 173.8 %reduce-scatter.50.cloned.1.call-start = ((), (), s32[]{:S(2)}) async-start(), calls=%async_computation.35 | async-start | bytes 1179648 | tf_op jit(solution)/shard_map/reduce_scatter | solution.py:361
  894.1 233.6 %reduce-scatter.46.cloned.1.call-start = ((), (), s32[]{:S(2)}) async-start(), calls=%async_computation.33 | async-start | bytes 294912 | tf_op jit(solution)/shard_map/reduce_scatter | solution.py:359
  897.6 294.0 %reduce-scatter.60.cloned.1.call-start = ((), (), s32[]{:S(2)}) async-start(), calls=%async_computation.40 | async-start | bytes 294912
  900.7 355.0 %reduce-scatter.44.cloned.1.call-start = ((), (), s32[]{:S(2)}) async-start(), calls=%async_computation.32 | async-start | bytes 294912 | tf_op jit(solution)/shard_map/reduce_scatter | solution.py:356
  903.9 416.1 %reduce-scatter.58.cloned.1.call-start = ((), (), s32[]{:S(2)}) async-start(), calls=%async_computation.39 | async-start | bytes 294912
  908.7 457.8 %reduce-scatter.40.cloned.1.call-start = ((), (), s32[]{:S(2)}) async-start(), calls=%async_computation.30 | async-start | bytes 5242880 | tf_op jit(solution)/shard_map/reduce_scatter | solution.py:84
  912.4 519.7 %reduce-scatter.42.cloned.1.call-start = ((), (), s32[]{:S(2)}) async-start(), calls=%async_computation.31 | async-start | bytes 294912 | tf_op jit(solution)/shard_map/reduce_scatter | solution.py:355
  916.7 580.0 %reduce-scatter.56.cloned.1.call-start = ((), (), s32[]{:S(2)}) async-start(), calls=%async_computation.38 | async-start | bytes 294912
  918.1 643.1 %reduce-scatter.52.cloned.1.call-start = ((), (), s32[]{:S(2)}) async-start(), calls=%async_computation.36 | async-start | bytes 294912
  920.6 705.1 %reduce-scatter.54.cloned.1.call-start = ((), (), s32[]{:S(2)}) async-start(), calls=%async_computation.37 | async-start | bytes 294912
  (97 other events, 2694.9 us)
Sparse Core Ops, SparseCore 0:
  9.6 25.2 all-gather.7
  185.1 45.3 reduce-scatter.27
  232.2 22.5 all-gather.11
  256.9 22.5 all-gather.9
  398.0 44.5 reduce-scatter.29
  445.6 22.5 all-gather.13
  526.5 44.6 reduce-scatter.31
  577.8 22.5 all-gather.15
  611.9 44.5 reduce-scatter.33
  661.0 22.5 all-gather.17
  742.7 44.5 reduce-scatter.35
  791.4 22.5 all-gather.19
  884.9 44.4 reduce-scatter.37
  933.2 63.5 reduce-scatter.47
  1001.0 62.4 reduce-scatter.49
  1067.3 60.2 reduce-scatter.45
  1131.4 60.2 reduce-scatter.59
  1195.4 60.2 reduce-scatter.43
  1259.7 60.2 reduce-scatter.57
  1322.9 43.5 reduce-scatter.39
  1370.8 61.2 reduce-scatter.41
  1436.3 60.2 reduce-scatter.55
  1500.9 60.2 reduce-scatter.51
  1565.4 60.2 reduce-scatter.53
where the time goes:
time: 1640 us; the launch traced here: 1630 us
  waiting for transfers between devices  951 us (58%)
  blocking collectives  354 us (22%)
  matrix products  138 us (8%)
  local copies, waits for them, and re-layouts  91.9 us (6%)
  other arithmetic  53.1 us (3%)
  loops' own time  27.4 us (2%)
    unnamed x29, waiting for transfers between devices  324 us
    reduce_scatter x4, waiting for transfers between devices, input_sum(): return lax.psum_scatter(total, 'tensor', scatter_dimension=0, tiled=True)  142 us
    reduce_scatter x3, waiting for transfers between devices, branch_sum(): lax.psum_scatter(jnp.dot(mixed, weight, preferred_element_type=jnp.float3...  133 us
    all_gather x3, waiting for transfers between devices, grad_rows(): return lax.all_gather(value, 'tensor', axis=0, tiled=True)  67.9 us
    reduce_scatter x1, waiting for transfers between devices, shards(): lax.psum_scatter(down_grad, 'dp', scatter_dimension=1, tiled=True)  66.7 us
    reduce_scatter x1, waiting for transfers between devices, shards(): lax.psum_scatter(self_output_grad, 'dp', scatter_dimension=1, tiled=True)  65.6 us
    reduce_scatter x1, waiting for transfers between devices, shards(): lax.psum_scatter(cross_query_grad, 'dp', scatter_dimension=0, tiled=True)  64.1 us
    reduce_scatter x1, waiting for transfers between devices, shards(): lax.psum_scatter(cross_output_grad, 'dp', scatter_dimension=1, tiled=True)  64.1 us
  transfers between devices with their start and end apart: 24, of which 20 were waited for; matrix products, arithmetic and copies ran while one was open for 3% of the time, Pallas kernels for 0%

commit v1 on v0

--- a/solution.py
+++ b/solution.py
@@ -8,6 +8,22 @@
 BLK = 128
 norm_eps = 1e-05
 mask_fill = -1000000000.0
+
+
+def collect(x, axis, dim):
+    ways, here, step = (lax.axis_size(axis), lax.axis_index(axis), x.shape[dim])
+    shape = [n * ways if d == dim else n for d, n in enumerate(x.shape)]
+    full = lax.dynamic_update_slice_in_dim(jnp.zeros(shape, x.dtype), x, here * step, axis=dim)
+    going_up = going_down = x
+    for far in range(1, ways // 2 + 1):
+        going_up = lax.ppermute(going_up, axis, [(d, (d + 1) % ways) for d in range(ways)])
+        full = lax.dynamic_update_slice_in_dim(full, going_up, (here - far) % ways * step, axis=dim)
+        if 2 * far < ways:
+            going_down = lax.ppermute(going_down, axis, [(d, (d - 1) % ways) for d in range(ways)])
+            full = lax.dynamic_update_slice_in_dim(
+                full, going_down, (here + far) % ways * step, axis=dim
+            )
+    return full
 
 
 def gelu_exact(value):
@@ -52,7 +68,7 @@
 
 
 def grad_rows(value):
-    return lax.all_gather(value, "tensor", axis=0, tiled=True)
+    return collect(value, "tensor", 0)
 
 
 def branch_sum(mixed, weight):

time: 1640 us -> 1750 us (1.067)
  matrix products: 138 us -> 203 us
  local copies, waits for them, and re-layouts: 91.9 us -> 142 us
    all_gather x3 -> x0, waiting for transfers between devices: 67.9 us -> none  [grad_rows(): return lax.all_gather(value, 'tensor', axis=0, tiled=True)]
    ppermute x0 -> x9, waiting for transfers between devices: none -> 55.6 us  [the longest x6 55.6 us: collect(): lax.ppermute(going_up, axis, [(d, (d + 1) % ways) for d in range(ways)])]
    reduce_scatter x1, waiting for transfers between devices: 66.7 us -> 23.6 us  [shards(): lax.psum_scatter(down_grad, 'dp', scatter_dimension=1, tiled=True)]
    reduce_scatter x1, waiting for transfers between devices: 23.6 us -> 66.7 us  [shards(): lax.psum_scatter(up_grad, 'dp', scatter_dimension=0, tiled=True)]
    squeeze x28, local copies, waits for them, and re-layouts: 8.29 us -> 31.9 us  [attend_all(): lax.map(one_sequence, (split_heads(query, count), split_heads(keys, count...]
    dot_general x16, matrix products: 13.8 us -> 33.4 us  [one_block(): jnp.einsum('qhd,khd->hqk', piece, keys, preferred_element_type=jnp.float32)]
    dot_general x8, matrix products: 12.9 us -> 31.6 us  [one_block(): jnp.einsum('qhd,khd->hqk', grad_piece, values, preferred_element_type=jnp...]
    unnamed x29 -> x26, waiting for transfers between devices: 324 us -> 323 us
  transfers between devices with their start and end apart: 24 -> 30, of which waited for: 20 -> 23; matrix products, arithmetic and copies ran while one was open for 3% -> 3% of each run, Pallas kernels for 0% -> 0%
where the time goes in v1:
time: 1750 us; the launch traced here: 1740 us
  waiting for transfers between devices  936 us (53%)
  blocking collectives  354 us (20%)
  matrix products  203 us (12%)
  local copies, waits for them, and re-layouts  142 us (8%)
  other arithmetic  50.6 us (3%)
  loops' own time  27.5 us (2%)
    unnamed x26, waiting for transfers between devices  323 us
    reduce_scatter x4, waiting for transfers between devices, input_sum(): return lax.psum_scatter(total, 'tensor', scatter_dimension=0, tiled=True)  140 us
    reduce_scatter x3, waiting for transfers between devices, branch_sum(): lax.psum_scatter(jnp.dot(mixed, weight, preferred_element_type=jnp.float3...  133 us
    reduce_scatter x1, waiting for transfers between devices, shards(): lax.psum_scatter(up_grad, 'dp', scatter_dimension=0, tiled=True)  66.7 us
    reduce_scatter x1, waiting for transfers between devices, shards(): lax.psum_scatter(self_output_grad, 'dp', scatter_dimension=1, tiled=True)  65.4 us
    reduce_scatter x1, waiting for transfers between devices, shards(): lax.psum_scatter(cross_output_grad, 'dp', scatter_dimension=1, tiled=True)  64.1 us
    reduce_scatter x1, waiting for transfers between devices, shards(): lax.psum_scatter(cross_query_grad, 'dp', scatter_dimension=0, tiled=True)  64.1 us
    ppermute x6, waiting for transfers between devices, collect(): lax.ppermute(going_up, axis, [(d, (d + 1) % ways) for d in range(ways)])  55.6 us
  transfers between devices with their start and end apart: 30, of which 23 were waited for; matrix products, arithmetic and copies ran while one was open for 3% of the time, Pallas kernels for 0%

profile of v1, /device:TPU:0, one launch (start us, length us, event | category | flops | bytes accessed | tf_op | source)
XLA Modules:
  0.0 1736.2 jit_solution(13358180007152276099)
XLA Ops:
  102.1 32.7 %all_gather.46 = bf16[128,512]{0,1:T(8,128)(2,1)} all-gather(bf16[128,64]{0,1:T(8,128)(2,1)} %param.47), channel_id=1, replica_groups=mesh['dp'=8,'tensor'=4] {'dp'}, dimensions={1}, use_global_device_ids=true | all-gather | bytes 147456 | tf_op jit(solution)/shard_map/all_gather | solution.py:263
  152.4 33.2 %while.147 = (s32[]{:T(128)}, bf16[2,1024,2,64]{3,2,1,0:T(2,128)(2,1)S(1)}, f32[2,2,2,512]{3,2,1,0:T(2,128)}, bf16[2,1024,2,64]{1,3,2,0:T(8,128)(2,1)}, bf16[2,1...) while((s32[]{:T(128)}, ...), condition=%wide.region_5.6_spmd, body=%wide.region_0.5_spmd.sunk | while | flops 283720704 | bytes 18707520 | solution.py:184
  189.9 44.5 %reduce-scatter.28.cloned.1.call-done = f32[512,512]{1,0:T(8,128)} async-done(((f32[2048,512]{1,0:T(8,128)}), f32[512,512]{1,0:T(8,128)}) %reduce-scatter.28.cloned.1.call-update) | async-done | bytes 1048592 | tf_op jit(solution)/shard_map/reduce_scatter | solution.py:75
  406.2 44.6 %reduce-scatter.30.cloned.1.call-done = f32[512,512]{1,0:T(8,128)} async-done(((f32[2048,512]{1,0:T(8,128)}), f32[512,512]{1,0:T(8,128)}) %reduce-scatter.30.cloned.1.call-update) | async-done | bytes 1048592 | tf_op jit(solution)/shard_map/reduce_scatter | solution.py:75
  535.4 44.2 %reduce-scatter.32.cloned.1.call-done = f32[512,512]{1,0:T(8,128)} async-done(((f32[2048,512]{1,0:T(8,128)}), f32[512,512]{1,0:T(8,128)}) %reduce-scatter.32.cloned.1.call-update) | async-done | bytes 1048592 | tf_op jit(solution)/shard_map/reduce_scatter | solution.py:75
  621.7 44.4 %reduce-scatter.34.cloned.1.call-done = f32[512,512]{1,0:T(8,128)} async-done(((f32[2048,512]{1,0:T(8,128)}), f32[512,512]{1,0:T(8,128)}) %reduce-scatter.34.cloned.1.call-update) | async-done | bytes 1048592 | tf_op jit(solution)/shard_map/reduce_scatter | solution.py:100
  702.9 87.1 %while.151 = (s32[]{:T(128)}, bf16[2,1024,2,64]{3,2,1,0:T(2,128)(2,1)}, bf16[2,1024,2,64]{1,3,2,0:T(8,128)(2,1)}, bf16[2,1024,2,64]{1,3,2,0:T(8,128)(2,1)}, bf16...) while((s32[]{:T(128)}, ...), condition=%wide.region_30.31_spmd, body=%wide.region_26.30_spmd.sunk | while | flops 684719104 | bytes 73578608 | solution.py:205
  709.7 33.5 %while.156 = (s32[]{:T(128)}, f32[1024,2,64]{0,2,1:T(8,128)S(1)}, f32[1024,2,64]{0,2,1:T(8,128)S(1)}, bf16[2,512,2,64]{1,3,2,0:T(8,128)(2,1)}, s32[2]{0:T(128)S(...) while((s32[]{:T(128)}, f32[1024,2,64]{0,2,1:T(8,128)S(1)}, ...), condition=%wide.region_29.29_spmd.clone, body=%wide.region_27.28_spmd.clone.sunk | while | flops 684456960 | bytes 68580160 | solution.py:168
  753.2 33.5 %while.156 = (s32[]{:T(128)}, f32[1024,2,64]{0,2,1:T(8,128)S(1)}, f32[1024,2,64]{0,2,1:T(8,128)S(1)}, bf16[2,512,2,64]{1,3,2,0:T(8,128)(2,1)}, s32[2]{0:T(128)S(...) while((s32[]{:T(128)}, f32[1024,2,64]{0,2,1:T(8,128)S(1)}, ...), condition=%wide.region_29.29_spmd.clone, body=%wide.region_27.28_spmd.clone.sunk | while | flops 684456960 | bytes 68580160 | solution.py:168
  795.3 44.4 %reduce-scatter.36.cloned.1.call-done = f32[512,512]{1,0:T(8,128)} async-done(((f32[2048,512]{1,0:T(8,128)}), f32[512,512]{1,0:T(8,128)}) %reduce-scatter.36.cloned.1.call-update) | async-done | bytes 1048592 | tf_op jit(solution)/shard_map/reduce_scatter | solution.py:100
  875.5 102.7 %while.153 = (s32[]{:T(128)}, bf16[2,1024,2,64]{3,2,1,0:T(2,128)(2,1)}, bf16[2,1024,2,64]{1,3,2,0:T(8,128)(2,1)}, bf16[2,1024,2,64]{1,3,2,0:T(8,128)(2,1)}, bf16...) while((s32[]{:T(128)}, ...), condition=%wide.region_38.39_spmd, body=%wide.region_34.38_spmd.sunk | while | flops 690502656 | bytes 82012608 | solution.py:205
  882.6 39.8 %while.157 = (s32[]{:T(128)}, f32[1024,2,64]{0,2,1:T(8,128)S(1)}, f32[1024,2,64]{0,2,1:T(8,128)}, bf16[2,512,2,64]{1,3,2,0:T(8,128)(2,1)}, s32[2]{0:T(128)}, /*i...) while((s32[]{:T(128)}, f32[1024,2,64]{0,2,1:T(8,128)S(1)}, ...), condition=%wide.region_37.37_spmd.clone, body=%wide.region_35.36_spmd.clone.sunk | while | flops 690240512 | bytes 77005864 | solution.py:168
  933.8 39.9 %while.157 = (s32[]{:T(128)}, f32[1024,2,64]{0,2,1:T(8,128)S(1)}, f32[1024,2,64]{0,2,1:T(8,128)}, bf16[2,512,2,64]{1,3,2,0:T(8,128)(2,1)}, s32[2]{0:T(128)}, /*i...) while((s32[]{:T(128)}, f32[1024,2,64]{0,2,1:T(8,128)S(1)}, ...), condition=%wide.region_37.37_spmd.clone, body=%wide.region_35.36_spmd.clone.sunk | while | flops 690240512 | bytes 77005864 | solution.py:168
  1036.3 39.9 %all-reduce = (f32[6,512]{1,0:T(8,128)}, f32[2,512]{1,0:T(2,128)S(1)}) all-reduce(f32[6,512]{1,0:T(8,128)S(1)} %stack.36, f32[2,512]{1,0:T(2,128)S(1)} %pad_maximum_fusion), channel_id=1, replica_groups=mesh['dp'=8,'tensor'=4] {'dp','tensor'}, use_global_device_ids=true, to_apply=%region_57.58 | all-reduce | flops 4096 | bytes 32768 | tf_op jit(solution)/shard_map/psum | solution.py:379
  1100.4 66.7 %reduce-scatter.48.cloned.1.call-done = f32[64,512]{1,0:T(8,128)} async-done(((f32[512,512]{1,0:T(8,128)}), f32[64,512]{1,0:T(8,128)}) %reduce-scatter.48.cloned.1.call-update) | async-done | bytes 131088 | tf_op jit(solution)/shard_map/reduce_scatter | solution.py:376
  1167.1 64.1 %reduce-scatter.46.cloned.1.call-done = f32[128,64]{0,1:T(8,128)} async-done(((f32[128,512]{0,1:T(8,128)}), f32[128,64]{0,1:T(8,128)}) %reduce-scatter.46.cloned.1.call-update) | async-done | bytes 32784 | tf_op jit(solution)/shard_map/reduce_scatter | solution.py:375
  1231.3 64.1 %reduce-scatter.44.cloned.1.call-done = f32[64,128]{1,0:T(8,128)} async-done(((f32[512,128]{1,0:T(8,128)}), f32[64,128]{1,0:T(8,128)}) %reduce-scatter.44.cloned.1.call-update) | async-done | bytes 32784 | tf_op jit(solution)/shard_map/reduce_scatter | solution.py:372
  1295.3 64.1 %reduce-scatter.58.cloned.1.call-done = f32[64,128]{1,0:T(8,128)} async-done(((f32[512,128]{1,0:T(8,128)}), f32[64,128]{1,0:T(8,128)}) %reduce-scatter.58.cloned.1.call-update) | async-done | bytes 32784
  1359.4 64.1 %reduce-scatter.60.cloned.1.call-done = f32[64,128]{1,0:T(8,128)} async-done(((f32[512,128]{1,0:T(8,128)}), f32[64,128]{1,0:T(8,128)}) %reduce-scatter.60.cloned.1.call-update) | async-done | bytes 32784
  1423.5 46.5 %reduce-scatter.40.cloned.1.call-done = f32[512,512]{1,0:T(8,128)} async-done(((f32[2048,512]{1,0:T(8,128)}), f32[512,512]{1,0:T(8,128)}) %reduce-scatter.40.cloned.1.call-update) | async-done | bytes 1048592 | tf_op jit(solution)/shard_map/reduce_scatter | solution.py:100
  1469.9 65.4 %reduce-scatter.42.cloned.1.call-done = f32[128,64]{0,1:T(8,128)} async-done(((f32[128,512]{0,1:T(8,128)}), f32[128,64]{0,1:T(8,128)}) %reduce-scatter.42.cloned.1.call-update) | async-done | bytes 32784 | tf_op jit(solution)/shard_map/reduce_scatter | solution.py:371
  1535.3 64.6 %reduce-scatter.54.cloned.1.call-done = f32[64,128]{1,0:T(8,128)} async-done(((f32[512,128]{1,0:T(8,128)}), f32[64,128]{1,0:T(8,128)}) %reduce-scatter.54.cloned.1.call-update) | async-done | bytes 32784
  1599.9 64.4 %reduce-scatter.56.cloned.1.call-done = f32[64,128]{1,0:T(8,128)} async-done(((f32[512,128]{1,0:T(8,128)}), f32[64,128]{1,0:T(8,128)}) %reduce-scatter.56.cloned.1.call-update) | async-done | bytes 32784
  1664.3 64.6 %reduce-scatter.52.cloned.1.call-done = f32[64,128]{1,0:T(8,128)} async-done(((f32[512,128]{1,0:T(8,128)}), f32[64,128]{1,0:T(8,128)}) %reduce-scatter.52.cloned.1.call-update) | async-done | bytes 32784
  (677 shorter events, 833.8 us)
Async XLA Ops:
  7.2 127.6 %all-gather.5.cloned.1.call-start = ((), (), s32[]{:S(2)}) async-start(), calls=%async_computation.17 | async-start | bytes 2621440 | tf_op jit(solution)/shard_map/all_gather | solution.py:67
  7.9 226.5 %reduce-scatter.28.cloned.1.call-start = ((), (), s32[]{:S(2)}) async-start(), calls=%async_computation.18 | async-start | bytes 5242880 | tf_op jit(solution)/shard_map/reduce_scatter | solution.py:75
  188.9 173.7 %all-gather.9.cloned.1.call-start = ((), (), s32[]{:S(2)}) async-start(), calls=%async_computation.20 | async-start | bytes 2621440 | tf_op jit(solution)/shard_map/all_gather | solution.py:67
  189.7 183.6 %all-gather.7.cloned.1.call-start = ((), (), s32[]{:S(2)}) async-start(), calls=%async_computation.19 | async-start | bytes 2621440 | tf_op jit(solution)/shard_map/all_gather | solution.py:67
  238.5 212.4 %reduce-scatter.30.cloned.1.call-start = ((), (), s32[]{:S(2)}) async-start(), calls=%async_computation.21 | async-start | bytes 5242880 | tf_op jit(solution)/shard_map/reduce_scatter | solution.py:75
  406.2 110.8 %all-gather.11.cloned.1.call-start = ((), (), s32[]{:S(2)}) async-start(), calls=%async_computation.22 | async-start | bytes 2621440 | tf_op jit(solution)/shard_map/all_gather | solution.py:67
  453.8 125.8 %reduce-scatter.32.cloned.1.call-start = ((), (), s32[]{:S(2)}) async-start(), calls=%async_computation.23 | async-start | bytes 5242880 | tf_op jit(solution)/shard_map/reduce_scatter | solution.py:75
  534.7 131.3 %reduce-scatter.34.cloned.1.call-start = ((), (), s32[]{:S(2)}) async-start(), calls=%async_computation.24 | async-start | bytes 5242880 | tf_op jit(solution)/shard_map/reduce_scatter | solution.py:100
  585.6 15.9 collective-permute-start.1
  621.7 218.0 %reduce-scatter.36.cloned.1.call-start = ((), (), s32[]{:S(2)}) async-start(), calls=%async_computation.25 | async-start | bytes 5242880 | tf_op jit(solution)/shard_map/reduce_scatter | solution.py:100
  671.7 14.7 collective-permute-start.4
  795.2 237.7 %reduce-scatter.38.cloned.1.call-start = ((), (), s32[]{:S(2)}) async-start(), calls=%async_computation.26 | async-start | bytes 5242880 | tf_op jit(solution)/shard_map/reduce_scatter | solution.py:100
  843.8 14.1 collective-permute-start.7
  988.6 111.9 %reduce-scatter.50.cloned.1.call-start = ((), (), s32[]{:S(2)}) async-start(), calls=%async_computation.32 | async-start | bytes 1179648 | tf_op jit(solution)/shard_map/reduce_scatter | solution.py:377
  994.1 173.0 %reduce-scatter.48.cloned.1.call-start = ((), (), s32[]{:S(2)}) async-start(), calls=%async_computation.31 | async-start | bytes 1179648 | tf_op jit(solution)/shard_map/reduce_scatter | solution.py:376
  999.0 232.3 %reduce-scatter.46.cloned.1.call-start = ((), (), s32[]{:S(2)}) async-start(), calls=%async_computation.30 | async-start | bytes 294912 | tf_op jit(solution)/shard_map/reduce_scatter | solution.py:375
  1002.5 292.8 %reduce-scatter.44.cloned.1.call-start = ((), (), s32[]{:S(2)}) async-start(), calls=%async_computation.29 | async-start | bytes 294912 | tf_op jit(solution)/shard_map/reduce_scatter | solution.py:372
  1005.6 353.8 %reduce-scatter.58.cloned.1.call-start = ((), (), s32[]{:S(2)}) async-start(), calls=%async_computation.36 | async-start | bytes 294912
  1008.7 414.7 %reduce-scatter.60.cloned.1.call-start = ((), (), s32[]{:S(2)}) async-start(), calls=%async_computation.37 | async-start | bytes 294912
  1013.5 456.5 %reduce-scatter.40.cloned.1.call-start = ((), (), s32[]{:S(2)}) async-start(), calls=%async_computation.27 | async-start | bytes 5242880 | tf_op jit(solution)/shard_map/reduce_scatter | solution.py:100
  1017.0 518.3 %reduce-scatter.42.cloned.1.call-start = ((), (), s32[]{:S(2)}) async-start(), calls=%async_computation.28 | async-start | bytes 294912 | tf_op jit(solution)/shard_map/reduce_scatter | solution.py:371
  1021.3 578.5 %reduce-scatter.54.cloned.1.call-start = ((), (), s32[]{:S(2)}) async-start(), calls=%async_computation.34 | async-start | bytes 294912
  1023.1 641.2 %reduce-scatter.56.cloned.1.call-start = ((), (), s32[]{:S(2)}) async-start(), calls=%async_computation.35 | async-start | bytes 294912
  1025.5 703.3 %reduce-scatter.52.cloned.1.call-start = ((), (), s32[]{:S(2)}) async-start(), calls=%async_computation.33 | async-start | bytes 294912
  (127 other events, 2914.9 us)
Sparse Core Ops, SparseCore 0:
  9.6 25.2 all-gather.4
  189.0 45.3 reduce-scatter.27
  236.1 22.5 all-gather.8
  260.8 22.5 all-gather.6
  406.3 44.5 reduce-scatter.29
  453.9 22.5 all-gather.10
  534.8 44.6 reduce-scatter.31
  621.8 44.2 reduce-scatter.33
  795.3 44.2 reduce-scatter.35
  988.7 44.1 reduce-scatter.37
  1036.9 63.4 reduce-scatter.49
  1104.7 62.4 reduce-scatter.47
  1171.0 60.2 reduce-scatter.45
  1235.0 60.2 reduce-scatter.43
  1299.1 60.2 reduce-scatter.57
  1363.2 60.2 reduce-scatter.59
  1426.4 43.4 reduce-scatter.39
  1474.1 61.2 reduce-scatter.41
  1539.6 60.2 reduce-scatter.53
  1604.0 60.2 reduce-scatter.55
  1668.5 60.2 reduce-scatter.51
